TPU v7x, 32 devices: a whole 2x2x4 slice. The times are simulated.
32 devices in a mesh: parts: 2 (over x), wide: 16 (over z, y, core).
Axes of the slice: x: 2, y: 2, z: 4, core: 2. Of those that a mesh axis runs over, the one named last changes fastest.
Arguments:
- tokens: bfloat16 [384, 7168], P(('parts', 'wide')), parts along dimension 0, may hold values from -6 to 6
- expert_ids: int32 [384, 8], P(('parts', 'wide')), parts along dimension 0, may hold values from 0 to 15, as said below
- gates: float32 [384, 8], P(('parts', 'wide')), parts along dimension 0, may hold values from 0.1 to 1
- w_gate: bfloat16 [2, 7168, 8192], P(None, None, 'wide'), may hold values from -0.0625 to 0.0625
- w_up: bfloat16 [2, 7168, 8192], P(None, None, 'wide'), may hold values from -0.0625 to 0.0625
- w_down: bfloat16 [2, 8192, 7168], P(None, 'wide'), may hold values from -0.1875 to 0.1875
Outputs:
- moe_out: bfloat16 [384, 7168], P(('parts', 'wide')), parts along dimension 0
There are 2 independent parts, one for each index of `parts`. A program takes and returns all parts, laid end to end along the dimension named above; an argument that names none is the same for every part. Nothing has to cross between parts.
Inputs may be any that keep to these rules, and one draw needn't show every extreme that they name: `expert_ids`: each row names the 2 experts g * 2 to g * 2 + 1 of each of 4 different groups g, in any order; in each part one group is named by every row.
All inputs are finite; a program needn't handle non-finite values.
Results may differ from a plain program's by a relative error of at most 0.0064.
Values may be sent and summed in bfloat16 or wider, within the bound.
A program may use at most 128 MiB of HBM per device.

v0:
```python
import functools
import math

import jax
import jax.numpy as jnp
from jax import lax
from jax.experimental import pallas as pl
from jax.experimental.pallas import tpu as pltpu
from jax.sharding import PartitionSpec as P

GROUPS = 8
EXP_G = 2
CORES = 2
SIDES = 2
CHUNK = 256
LANES = 128
LAG_SIDE = 3
LAG_USE = 4
LAG_SUM = 1
LAG_Z = 4
LAG_END = 7
F32 = jnp.float32
BF16 = jnp.bfloat16


def floor_div(value, by):
    return jnp.floor((value + 0.5) * (1.0 / by))


def iota_f32(shape, dim):
    return lax.broadcasted_iota(jnp.int32, shape, dim).astype(F32)


def kernel(
    wide, rows, fold,
    tok_ref, ids_ref, gate_ref, wg_ref, wu_ref, wd_ref, out_ref,
    tok, x_ref, r_ref, xb, rb, wgb, wub, wdb, acc, hid, perm, perm_back, packed, got_core, sum_side, got_side, sum_z, got_z,
    tok_sem, w_sem, d_sem, own_sem, az_s, az_r, ay_s, ay_r, ac_s, ac_r, bz_s, bz_r, by_s, by_r, bc_s, bc_r,
):
    zs = wide // (CORES * SIDES)
    chunks = x_ref.shape[0]
    hidden = wg_ref.shape[2]
    width = chunks * CHUNK
    unit = rows * fold
    units = wide
    groups = units // fold
    band = fold * rows
    pad_rows = r_ref.shape[0]

    me = lax.axis_index("wide")
    core = lax.rem(me, CORES)
    chip = me // CORES
    side = lax.rem(chip, SIDES)
    z = chip // SIDES
    other_core = 1 - core
    other_side = 1 - side

    def at(z_at, side_at, core_at):
        return {"wide": (z_at * SIDES + side_at) * CORES + core_at}

    core_dev = at(z, side, other_core)
    side_dev = at(z, other_side, core)

    def z_of(step):
        return lax.rem(z + step, zs)

    def send(src, dst, s_sem, r_sem, dev):
        return pltpu.make_async_remote_copy(
            src_ref=src, dst_ref=dst, send_sem=s_sem, recv_sem=r_sem, device_id=dev, device_id_type=pl.DeviceIdType.MESH
        )

    def up_copies(k):
        copies = []
        for block in range(fold):
            source = pl.ds(pl.multiple_of(block * width + k * CHUNK, CHUNK), CHUNK)
            target = pl.ds(block * CHUNK, CHUNK)
            copies.append(pltpu.make_async_copy(wg_ref.at[:, source, :], wgb.at[k, :, target, :], w_sem.at[k, 2 * block]))
            copies.append(pltpu.make_async_copy(wu_ref.at[:, source, :], wub.at[k, :, target, :], w_sem.at[k, 2 * block + 1]))
        return copies

    def down_copies(k):
        copies = []
        for block in range(fold):
            source = pl.ds(pl.multiple_of(block * width + k * CHUNK, CHUNK), CHUNK)
            for expert in range(EXP_G):
                copies.append(pltpu.make_async_copy(
                    wd_ref.at[expert, :, source],
                    wdb.at[k, pl.ds(expert * hidden, hidden), pl.ds(block * CHUNK, CHUNK)],
                    d_sem.at[k, block * EXP_G + expert],
                ))
        return copies

    def own_z(k, step):
        return send(x_ref.at[k], xb.at[k, core, side, z], az_s.at[k, step], az_r.at[k, step], at(z_of(step), side, core))

    def side_hop(k, step):
        spot = xb.at[k, core, side, z_of(step)]
        source = x_ref.at[k] if step == 0 else spot
        return send(source, spot, ay_s.at[k, step], ay_r.at[k, step], side_dev)

    def core_hop(k, half, half_index):
        return send(xb.at[k, core, half], xb.at[k, core, half], ac_s.at[k, half_index], ac_r.at[k, half_index], core_dev)

    def own_local(k):
        return pltpu.make_async_copy(x_ref.at[k], xb.at[k, core, side, z], own_sem.at[k])

    def route_z(step):
        return send(r_ref, rb.at[core, side, z], az_s.at[chunks, step], az_r.at[chunks, step], at(z_of(step), side, core))

    def route_side():
        return send(rb.at[core, side], rb.at[core, side], ay_s.at[chunks, 0], ay_r.at[chunks, 0], side_dev)

    def route_core():
        return send(rb.at[core], rb.at[core], ac_s.at[chunks, 0], ac_r.at[chunks, 0], core_dev)

    def route_local():
        return pltpu.make_async_copy(r_ref, rb.at[core, side, z], own_sem.at[chunks])

    token_copy = pltpu.make_async_copy(tok_ref, tok, tok_sem)
    token_copy.start()
    for copy in up_copies(0):
        copy.start()

    barrier = pltpu.get_barrier_semaphore()
    for step in range(1, zs):
        pl.semaphore_signal(barrier, inc=1, device_id=at(z_of(step), side, core), device_id_type=pl.DeviceIdType.MESH)
    pl.semaphore_signal(barrier, inc=1, device_id=side_dev, device_id_type=pl.DeviceIdType.MESH)
    pl.semaphore_signal(barrier, inc=1, device_id=core_dev, device_id_type=pl.DeviceIdType.MESH)

    lane = lax.broadcasted_iota(jnp.int32, (rows, LANES), 1)
    route = jnp.zeros((rows, LANES), F32)
    for slot in range(ids_ref.shape[1]):
        route = route + jnp.where(ids_ref[:, slot:slot + 1] == lane, gate_ref[:, slot:slot + 1], 0.0)
    spread = (iota_f32((pad_rows, rows), 0) == iota_f32((pad_rows, rows), 1)).astype(F32).astype(BF16)
    r_ref[...] = jnp.dot(spread, route.astype(BF16), preferred_element_type=F32).astype(BF16)
    route_local().start()
    token_copy.wait()
    place = iota_f32((unit, rows), 0) - iota_f32((unit, rows), 1)
    into = [(place == block * rows).astype(F32).astype(BF16) for block in range(fold)]
    for k in range(chunks):
        parts = [jnp.dot(into[block], tok[:, block * width + k * CHUNK:block * width + (k + 1) * CHUNK], preferred_element_type=F32) for block in range(fold)]
        x_ref[k] = sum(parts[1:], parts[0]).astype(BF16)
        own_local(k).start()
        if k == 0:
            pl.semaphore_wait(barrier, zs + 1)
        side_hop(k, 0).start()
        for step in range(1, zs):
            own_z(k, step).start()
        if k == 0:
            for step in range(1, zs):
                route_z(step).start()
    size = fold * band
    def order(index):
        first = floor_div(index, band)
        rest = index - first * band
        second = floor_div(rest, rows)
        return second * band + first * rows + (rest - second * rows)

    perm[...] = (order(iota_f32((size, 1), 0)) == iota_f32((size, size), 1)).astype(F32).astype(BF16)
    perm_back[...] = (iota_f32((size, size), 0) == order(iota_f32((1, size), 1))).astype(F32).astype(BF16)
    acc[...] = jnp.zeros_like(acc)

    @pl.loop(0, chunks + LAG_USE)
    def _(now):
        @pl.when(now < chunks)
        def _():
            k = now
            for step in range(1, zs):
                back = zs - step
                send(x_ref.at[k], xb.at[k, core, side, z_of(back)], az_s.at[k, step], az_r.at[k, step], at(z_of(back), side, core)).wait_recv()
                side_hop(k, back).start()
            own_local(k).wait()
            core_hop(k, side, 0).start()

            @pl.when(k + 1 < chunks)
            def _():
                for copy in up_copies(k + 1):
                    copy.start()

            for copy in down_copies(k):
                copy.start()

            @pl.when(k == 0)
            def _():
                route_local().wait()
                for step in range(1, zs):
                    route_z(step).wait_recv()
                route_side().start()

        @pl.when((now >= LAG_SIDE) & (now < chunks + LAG_SIDE))
        def _():
            k = now - LAG_SIDE
            for step in range(zs):
                spot = xb.at[k, core, other_side, z_of(step)]
                send(spot, spot, ay_s.at[k, step], ay_r.at[k, step], side_dev).wait_recv()
            core_hop(k, other_side, 1).start()

            @pl.when(k == 0)
            def _():
                send(rb.at[core, other_side], rb.at[core, other_side], ay_s.at[chunks, 0], ay_r.at[chunks, 0], side_dev).wait_recv()
                route_core().start()

        @pl.when(now >= LAG_USE)
        def _():
            k = now - LAG_USE
            for half_index, half in ((0, side), (1, other_side)):
                spot = xb.at[k, other_core, half]
                send(spot, spot, ac_s.at[k, half_index], ac_r.at[k, half_index], core_dev).wait_recv()
            for copy in up_copies(k):
                copy.wait()
            folded = xb[k].reshape(groups, size, CHUNK)
            straight = []
            for group in range(groups):
                moved = jnp.dot(perm[...], folded[group], preferred_element_type=F32).astype(BF16)
                straight.append(jnp.concatenate([moved[block * band:(block + 1) * band] for block in range(fold)], axis=1))
            left = jnp.concatenate(straight, axis=0)
            for expert in range(EXP_G):
                acc[2 * expert] += jnp.dot(left, wgb[k, expert], preferred_element_type=F32)
                acc[2 * expert + 1] += jnp.dot(left, wub[k, expert], preferred_element_type=F32)

    route_core_spot = rb.at[other_core]
    send(route_core_spot, route_core_spot, ac_s.at[chunks, 0], ac_r.at[chunks, 0], core_dev).wait_recv()
    total = units * rows
    line = iota_f32((1, units * pad_rows), 1)
    unit_of = floor_div(line, pad_rows)
    row_of = line - unit_of * pad_rows
    wanted = jnp.where(row_of < rows, unit_of * rows + row_of, -1.0)
    pick = (iota_f32((total, units * pad_rows), 0) == wanted).astype(F32).astype(BF16)
    scales = jnp.dot(pick, rb[...].reshape(units * pad_rows, LANES), preferred_element_type=F32)
    lane = lax.broadcasted_iota(jnp.int32, (total, LANES), 1)
    first_expert = me // (wide // GROUPS) * EXP_G
    for expert in range(EXP_G):
        scale = jnp.sum(jnp.where(lane == first_expert + expert, scales, 0.0), axis=1, keepdims=True)
        gate = acc[2 * expert]
        value = gate / (1.0 + jnp.exp(-gate)) * acc[2 * expert + 1]
        hid[:, expert * hidden:(expert + 1) * hidden] = (value * scale).astype(BF16)

    def back_core(k):
        return send(packed.at[k, other_core], got_core.at[k], bc_s.at[k], bc_r.at[k], core_dev)

    def back_side(k):
        return send(sum_side.at[k, other_side], got_side.at[k], by_s.at[k], by_r.at[k], side_dev)

    def back_z(k, step):
        return send(sum_z.at[k, z_of(step)], got_z.at[k, step], bz_s.at[k, step], bz_r.at[k, step], at(z_of(step), side, core))

    @pl.loop(0, chunks + LAG_END)
    def _(now):
        @pl.when(now < chunks)
        def _():
            k = now
            for copy in down_copies(k):
                copy.wait()
            down = jnp.dot(hid[...], wdb[k], preferred_element_type=F32).astype(BF16)
            sets = []
            for group in range(groups):
                lines = down[group * band:(group + 1) * band]
                stacked = jnp.concatenate([lines[:, block * CHUNK:(block + 1) * CHUNK] for block in range(fold)], axis=0)
                sets.append(jnp.dot(perm_back[...], stacked, preferred_element_type=F32).astype(BF16))
            packed[k] = jnp.concatenate(sets, axis=0).reshape(CORES, SIDES, zs, unit, CHUNK)
            back_core(k).start()

        @pl.when((now >= LAG_SUM) & (now < chunks + LAG_SUM))
        def _():
            k = now - LAG_SUM
            back_core(k).wait_recv()
            sum_side[k] = (packed[k, core].astype(F32) + got_core[k].astype(F32)).astype(BF16)
            back_side(k).start()

        @pl.when((now >= LAG_Z) & (now < chunks + LAG_Z))
        def _():
            k = now - LAG_Z
            back_side(k).wait_recv()
            sum_z[k] = (sum_side[k, side].astype(F32) + got_side[k].astype(F32)).astype(BF16)
            for step in range(1, zs):
                back_z(k, step).start()

        @pl.when(now >= LAG_END)
        def _():
            k = now - LAG_END
            done = sum_z[k, z].astype(F32)
            for step in range(1, zs):
                back_z(k, step).wait_recv()
                done = done + got_z[k, step].astype(F32)
            final = done.astype(BF16)
            away = iota_f32((rows, unit), 1) - iota_f32((rows, unit), 0)
            for block in range(fold):
                out_of = (away == block * rows).astype(F32).astype(BF16)
                spot = pl.ds(pl.multiple_of(block * width + k * CHUNK, CHUNK), CHUNK)
                out_ref[:, spot] = jnp.dot(out_of, final, preferred_element_type=F32).astype(BF16)

    @pl.loop(0, chunks)
    def _(k):
        for step in range(1, zs):
            own_z(k, step).wait_send()
            back_z(k, step).wait_send()
        for step in range(zs):
            side_hop(k, step).wait_send()
        core_hop(k, side, 0).wait_send()
        core_hop(k, other_side, 1).wait_send()
        back_core(k).wait_send()
        back_side(k).wait_send()

    for step in range(1, zs):
        route_z(step).wait_send()
    route_side().wait_send()
    route_core().wait_send()


def local(wide, interpret, tokens, expert_ids, gates, w_gate, w_up, w_down):
    rows, model = tokens.shape
    hidden = w_gate.shape[2]
    fold = 16 // math.gcd(16, rows)
    width = model // fold
    chunks = width // CHUNK
    zs = wide // (CORES * SIDES)
    pad_rows = -(-rows // 16) * 16
    unit = rows * fold
    size = fold * unit
    total = wide * rows

    any_space = pl.BlockSpec(memory_space=pl.ANY)
    dma = pltpu.SemaphoreType.DMA
    out = pl.pallas_call(
        functools.partial(kernel, wide, rows, fold),
        out_shape=jax.ShapeDtypeStruct((rows, model), BF16),
        in_specs=[any_space] + [pl.BlockSpec(memory_space=pltpu.VMEM)] * 2 + [any_space] * 3,
        out_specs=pl.BlockSpec(memory_space=pltpu.VMEM),
        scratch_shapes=[
            pltpu.VMEM((rows, model), BF16),
            pltpu.VMEM((chunks, unit, CHUNK), BF16),
            pltpu.VMEM((pad_rows, LANES), BF16),
            pltpu.VMEM((chunks, CORES, SIDES, zs, unit, CHUNK), BF16),
            pltpu.VMEM((CORES, SIDES, zs, pad_rows, LANES), BF16),
            pltpu.VMEM((chunks, EXP_G, fold * CHUNK, hidden), BF16),
            pltpu.VMEM((chunks, EXP_G, fold * CHUNK, hidden), BF16),
            pltpu.VMEM((chunks, EXP_G * hidden, fold * CHUNK), BF16),
            pltpu.VMEM((2 * EXP_G, total, hidden), F32),
            pltpu.VMEM((total, EXP_G * hidden), BF16),
            pltpu.VMEM((size, size), BF16),
            pltpu.VMEM((size, size), BF16),
            pltpu.VMEM((chunks, CORES, SIDES, zs, unit, CHUNK), BF16),
            pltpu.VMEM((chunks, SIDES, zs, unit, CHUNK), BF16),
            pltpu.VMEM((chunks, SIDES, zs, unit, CHUNK), BF16),
            pltpu.VMEM((chunks, zs, unit, CHUNK), BF16),
            pltpu.VMEM((chunks, zs, unit, CHUNK), BF16),
            pltpu.VMEM((chunks, zs, unit, CHUNK), BF16),
            dma(()),
            dma((chunks, 2 * fold)),
            dma((chunks, EXP_G * fold)),
            dma((chunks + 1,)),
            dma((chunks + 1, zs)), dma((chunks + 1, zs)),
            dma((chunks + 1, zs)), dma((chunks + 1, zs)),
            dma((chunks + 1, 2)), dma((chunks + 1, 2)),
            dma((chunks, zs)), dma((chunks, zs)),
            dma((chunks,)), dma((chunks,)),
            dma((chunks,)), dma((chunks,)),
        ],
        compiler_params=pltpu.CompilerParams(collective_id=0, has_side_effects=True, vmem_limit_bytes=67043328),
        **interpret,
    )(tokens, expert_ids, gates, w_gate, w_up, w_down)
    return out


def solution(mesh, interpret=None):
    return jax.shard_map(
        functools.partial(local, mesh.shape["wide"], interpret or {}),
        mesh=mesh,
        in_specs=(
            P(("parts", "wide"), None),
            P(("parts", "wide"), None),
            P(("parts", "wide"), None),
            P(None, None, "wide"),
            P(None, None, "wide"),
            P(None, "wide", None),
        ),
        out_specs=P(("parts", "wide"), None),
        check_vma=False,
    )
```

profile of v0, /device:TPU:0, one launch (start us, length us, event | category | flops | bytes accessed | tf_op | source)
XLA Modules:
  0.0 62.4 jit_solution(14550612581904163750)
XLA Ops:
  0.0 1.4 %copy.7.ids_ref = s32[12,8]{1,0:T(8,128)} copy(s32[12,8]{0,1:T(8,128)} %param.7) | data formatting | bytes 768 | tf_op args[1]
  1.4 1.4 %copy.8.gate_ref = f32[12,8]{1,0:T(8,128)} copy(f32[12,8]{0,1:T(8,128)} %param.8) | data formatting | bytes 768 | tf_op args[2]
  2.7 58.0 %shard_map.64 = bf16[12,7168]{1,0:T(8,128)(2,1)} custom-call(bf16[12,7168]{1,0:T(8,128)(2,1)} %tok_ref.1, s32[12,8]{1,0:T(8,128)} %copy.7.ids_ref, f32[12,8]{1,0:T(8,128)} %copy.8.gate_ref, bf16[2,7168,512]{2,1,0:T(8,128)(2,1)} %wg_ref.1, bf16[2,7168,512]{2,1,0:T(8,128)(2,1)} %wu_ref.1, bf16[2,512,7168]{2,1,0:T(8,128)(2,1)} %wd_ref.1), custom_call_target="tpu_custom_call" | custom-call | tf_op jit(solution)/shard_map/pallas_call | solution.py:324
  60.7 1.6 %copy.10 = bf16[12,7168]{1,0:T(8,128)(2,1)} copy(bf16[12,7168]{1,0:T(8,128)(2,1)} %shard_map.64) | data formatting | bytes 344064
where the time goes:
time: 62.7 us; the launch traced here: 62.4 us
  Pallas kernels  58 us (93%)
  local copies, waits for them, and re-layouts  4.36 us (7%)
    pallas_call x1, Pallas kernels, local(): pl.pallas_call(functools.partial(kernel, wide, rows, fold), out_shape=jax...  58 us
    unnamed x3, local copies, waits for them, and re-layouts  4.36 us

commit v1 on v0

v1 whole, which is shorter than its diff:
```python
import functools
import math

import jax
import jax.numpy as jnp
from jax import lax
from jax.experimental import pallas as pl
from jax.experimental.pallas import tpu as pltpu
from jax.sharding import PartitionSpec as P

GROUPS = 8
EXP_G = 2
CORES = 2
SIDES = 2
LANES = 128
CHUNK = 256
BATCHES = 1
SPLIT = 0
AHEAD = 20
SPLIT_AHEAD = 0
LAG_RELAY = 0
LAG_SIDE = 2
LAG_USE = 3
LAG_SUM = 2
LAG_Z = 5
LAG_ZR = 5
LAG_END = 8
NEAR = 3
F32 = jnp.float32
BF16 = jnp.bfloat16


def floor_div(value, by):
    return jnp.floor((value + 0.5) * (1.0 / by))


def iota_f32(shape, dim):
    return lax.broadcasted_iota(jnp.int32, shape, dim).astype(F32)


def one_hot(match):
    return match.astype(F32).astype(BF16)


def kernel(
    wide, rows, batches, fold, split,
    tok_ref, ids_ref, gate_ref, wg_ref, wu_ref, wd_ref, out_ref,
    tok, padded, r_ref, xb, rb, wb, wdb, acc, hid, perm, perm_back, packed, got_core, red, got_side, got_z, relay, got_y, fin,
    tok_sem, own_sem, w_sem, d_sem, route_s, route_r, out_s, az_r, af_r, ay_r, ac_r, bc_r, by_r, bz_r, br_r,
):
    zs = wide // (CORES * SIDES)
    total = xb.shape[0]
    chunks = total // batches
    hidden = wg_ref.shape[2]
    part = rows // batches
    unit = part * fold
    span = fold * CHUNK
    units = wide
    groups = units // fold
    size = fold * unit
    lines = units * part
    pad_rows = r_ref.shape[0]
    near = range(1, min(NEAR, zs - 1) + 1)
    far = range(NEAR + 1, zs)
    extra = batches * split

    me = lax.axis_index("wide")
    core = lax.rem(me, CORES)
    chip = me // CORES
    side = lax.rem(chip, SIDES)
    z = chip // SIDES
    other_core = 1 - core
    other_side = 1 - side
    halves = (side, other_side)

    def at(z_at, side_at, core_at):
        return {"wide": (z_at * SIDES + side_at) * CORES + core_at}

    core_dev = at(z, side, other_core)
    side_dev = at(z, other_side, core)

    def inside(value):
        return (value >= 0) & (value < zs)

    def around(distances):
        return [(d, sign, z + sign * d, (d - 1) * 2 + (sign + 1) // 2) for d in distances for sign in (-1, 1)]

    def send(src, dst, s_sem, r_sem, dev):
        return pltpu.make_async_remote_copy(
            src_ref=src, dst_ref=dst, send_sem=s_sem, recv_sem=r_sem, device_id=dev, device_id_type=pl.DeviceIdType.MESH
        )

    def up_copies(k):
        rows_of = pl.ds(pl.multiple_of(k * span, span), span)
        return [
            pltpu.make_async_copy(wg_ref.at[:, rows_of, :], wb.at[k, pl.ds(0, EXP_G)], w_sem.at[k]),
            pltpu.make_async_copy(wu_ref.at[:, rows_of, :], wb.at[k, pl.ds(EXP_G, EXP_G)], w_sem.at[k]),
        ]

    def up_wait(k):
        pltpu.make_async_copy(wb.at[k], wb.at[k], w_sem.at[k]).wait()

    def down_copies(k):
        columns = pl.ds(pl.multiple_of(k * span, span), span)
        return [
            pltpu.make_async_copy(wd_ref.at[e, :, columns], wdb.at[k, pl.ds(e * hidden, hidden), :], d_sem.at[k])
            for e in range(EXP_G)
        ]

    def down_wait(k):
        pltpu.make_async_copy(wdb.at[k], wdb.at[k], d_sem.at[k]).wait()

    def line_of(q, rel, first):
        return q if rel == 0 else total + q // chunks * split + lax.rem(q, chunks) - first

    def by_count(pairs, rule, act):
        here = sum(rule(z + sign * d, z - sign).astype(jnp.int32) for d, sign in pairs)
        held_here = {sum(bool(rule(spot + sign * d, spot - sign)) for d, sign in pairs) for spot in range(zs)}
        for n in sorted(held_here - {0}):
            @pl.when(here == n)
            def _():
                act(n)

    def ends(distances):
        return [(d, sign) for d in distances for sign in (-1, 1)]

    def any_end(value, behind):
        return inside(value)

    def any_through(value, behind):
        return inside(value) & inside(behind)

    def any_first(value, behind):
        return inside(value) & ((behind < 0) | (behind >= zs))

    def z_hop(q, rel, src, dst, kind, r_sem):
        spot = xb.at[q, core, halves[rel], src]
        return send(spot, spot, out_s.at[kind], r_sem, at(dst, side, core))

    def y_hop(q, half, src, kind):
        spot = xb.at[q, core, half, src]
        return send(spot, spot, out_s.at[kind], ay_r.at[q], side_dev)

    def core_hop(q, owner, rel):
        spot = xb.at[q, owner, halves[rel]]
        return send(spot, spot, out_s.at[6], ac_r.at[q], core_dev)

    def z_own(q, rel):
        line = line_of(q, rel, chunks - split)
        for d, sign, dst, slot in reversed(around(near)):
            @pl.when(inside(dst))
            def _():
                z_hop(q, rel, z, dst, rel, az_r.at[line, slot]).start()

    def z_onward(q, rel, distances, onward):
        for d, sign, src, slot in around(distances):
            @pl.when(inside(src))
            def _():
                if d >= NEAR and d + 1 < zs:
                    @pl.when(inside(z - sign))
                    def _():
                        z_hop(q, rel, src, z - sign, 2 + rel, af_r.at[line_of(q, rel, chunks - split), d - NEAR]).start()
                if onward:
                    y_hop(q, side, src, 5).start()

    def z_wait(q, rel, distances, r_sem):
        def wait(n):
            spot = xb.at[q, core, halves[rel], pl.ds(0, n)]
            send(spot, spot, out_s.at[0], r_sem, core_dev).wait_recv()

        by_count(ends(distances), any_end, wait)

    def arrive_near(q, rel, onward):
        line = line_of(q, rel, chunks - split)
        for d, sign, src, slot in around(near):
            @pl.when(inside(z - sign * d))
            def _():
                z_hop(q, rel, z - sign * d, z - sign * d, 0, az_r.at[line, slot]).wait_recv()
                if d >= NEAR and d + 1 < zs:
                    @pl.when(inside(z + sign))
                    def _():
                        z_hop(q, rel, z - sign * d, z + sign, 2 + rel, af_r.at[line, d - NEAR]).start()
                if onward:
                    y_hop(q, side, z - sign * d, 5).start()

    def arrive_far(q, rel, onward):
        for d in far:
            z_wait(q, rel, [d], af_r.at[line_of(q, rel, chunks - split), d - NEAR - 1])
            z_onward(q, rel, [d], onward)

    def route_z(step):
        dst = lax.rem(z + step, zs)
        return send(r_ref, rb.at[core, side, z], route_s.at[0], route_r.at[step], at(dst, side, core))

    def route_side(half):
        return send(rb.at[core, half], rb.at[core, half], route_s.at[1], route_r.at[zs], side_dev)

    def route_core(owner):
        return send(rb.at[owner], rb.at[owner], route_s.at[2], route_r.at[zs + 1], core_dev)

    def route_local():
        return pltpu.make_async_copy(r_ref, rb.at[core, side, z], own_sem)

    def back_core(p):
        return send(packed.at[p, other_core], got_core.at[p], out_s.at[7], bc_r.at[p], core_dev)

    def back_side(p):
        return send(red.at[p, 1], got_side.at[p], out_s.at[8], by_r.at[p], side_dev)

    def back_last(p):
        return send(got_y.at[p, 0], got_y.at[p, 1], out_s.at[9], by_r.at[p], side_dev)

    def back_z(p, rel, dst, slot):
        r_sem = bz_r.at[line_of(p, rel, 0)]
        return send(red.at[p, rel, dst], got_z.at[p, rel, slot], out_s.at[10 + rel], r_sem, at(dst, side, core))

    def back_relay(p, rel, d, dst, to):
        r_sem = br_r.at[line_of(p, rel, 0), d]
        return send(red.at[p, rel, dst], relay.at[p, rel, dst], out_s.at[12 + rel], r_sem, at(to, side, core))

    def reduce_out(p, rel, d, sign, dst, slot):
        if d <= NEAR:
            back_z(p, rel, dst, slot).start()
        else:
            back_relay(p, rel, d - NEAR - 1, dst, z + sign).start()

    def reduce_first(p, rel):
        for d, sign, dst, slot in reversed(around(range(1, zs))):
            ready = inside(dst) if d < NEAR else any_first(dst, z - sign)

            @pl.when(ready)
            def _():
                reduce_out(p, rel, d, sign, dst, slot)

    def reduce_second(p, rel):
        for d in reversed(range(NEAR, zs - 1)):
            def wait(n):
                spot = relay.at[p, rel, pl.ds(0, n)]
                send(spot, spot, out_s.at[0], br_r.at[line_of(p, rel, 0), d - NEAR], core_dev).wait_recv()

            by_count(ends([d]), any_through, wait)
            for _, sign, dst, slot in around([d]):
                @pl.when(any_through(dst, z - sign))
                def _():
                    red[p, rel, dst] = (red[p, rel, dst].astype(F32) + relay[p, rel, dst].astype(F32)).astype(BF16)
                    reduce_out(p, rel, d, sign, dst, slot)

    def reduce_last(p, rel):
        def wait(n):
            spot = got_z.at[p, rel, pl.ds(0, n)]
            send(spot, spot, out_s.at[0], bz_r.at[line_of(p, rel, 0)], core_dev).wait_recv()

        by_count(ends(near), any_end, wait)
        done = red[p, rel, z].astype(F32)
        for d, sign, src, slot in around(near):
            done = done + got_z[p, rel, slot].astype(F32)
        return done

    token_copy = pltpu.make_async_copy(tok_ref, tok, tok_sem)
    token_copy.start()
    for copy in up_copies(0):
        copy.start()

    for d, sign, src, slot in around(near):
        @pl.when(jnp.logical_not(inside(z - sign * d)))
        def _():
            @pl.loop(0, total)
            def _(p):
                for rel in range(SIDES):
                    got_z[p, rel, slot] = jnp.zeros((unit, CHUNK), BF16)

    barrier = pltpu.get_barrier_semaphore()
    for step in range(1, zs):
        pl.semaphore_signal(barrier, inc=1, device_id=at(lax.rem(z + step, zs), side, core), device_id_type=pl.DeviceIdType.MESH)
    pl.semaphore_signal(barrier, inc=1, device_id=side_dev, device_id_type=pl.DeviceIdType.MESH)
    pl.semaphore_signal(barrier, inc=1, device_id=core_dev, device_id_type=pl.DeviceIdType.MESH)

    def place(index):
        batch = floor_div(index, unit)
        rest = index - batch * unit
        block = floor_div(rest, part)
        return block * pad_rows + batch * part + rest - block * part

    held = batches * unit
    into = one_hot(iota_f32((held, fold * pad_rows), 1) == place(iota_f32((held, 1), 0)))
    spread = one_hot(iota_f32((pad_rows, rows), 0) == iota_f32((pad_rows, rows), 1))
    token_copy.wait()
    padded[...] = jnp.dot(spread, tok[...], preferred_element_type=F32).astype(BF16)

    def pack(k):
        tiles = jnp.concatenate([padded[:, k * span + f * CHUNK:k * span + (f + 1) * CHUNK] for f in range(fold)], axis=0)
        mine = jnp.dot(into, tiles, preferred_element_type=F32).astype(BF16)
        for b in range(batches):
            xb[b * chunks + k, core, side, z] = mine[b * unit:(b + 1) * unit]

    def offer(q):
        y_hop(q, side, z, 4).start()
        z_own(q, 0)

    token = lax.broadcasted_iota(jnp.int32, (LANES, rows), 0)
    route = jnp.zeros((LANES, rows), F32)
    for slot in range(ids_ref.shape[0]):
        route = route + jnp.where(ids_ref[slot:slot + 1, :] == token, gate_ref[slot:slot + 1, :], 0.0)
    r_ref[...] = lax.dot_general(spread, route.astype(BF16), (((1,), (1,)), ((), ())), preferred_element_type=F32).astype(BF16)
    route_local().start()
    pack(0)
    pl.semaphore_wait(barrier, zs + 1)
    offer(0)
    for step in range(1, zs):
        route_z(step).start()
    for k in range(1, chunks):
        pack(k)
        if k < AHEAD:
            offer(k)
    for q in range(chunks, min(AHEAD, total)):
        offer(q)

    def order(index):
        first = floor_div(index, unit)
        rest = index - first * unit
        second = floor_div(rest, part)
        return second * unit + first * part + (rest - second * part)

    perm[...] = one_hot(order(iota_f32((size, 1), 0)) == iota_f32((size, size), 1))
    perm_back[...] = one_hot(iota_f32((size, size), 0) == order(iota_f32((1, size), 1)))
    acc[...] = jnp.zeros_like(acc)

    lag_down = LAG_USE + chunks - 1

    def staged(lag, count=total):
        def wrap(body):
            def run(now):
                @pl.when((now >= lag) & (now < count + lag))
                def _():
                    body(now - lag)
            return run
        return wrap

    def either(test, yes, no):
        if split == 0:
            no()
        else:
            pl.when(test)(yes)
            pl.when(jnp.logical_not(test))(no)

    def gather_split(q):
        return lax.rem(q, chunks) >= chunks - split

    def scatter_split(p):
        return lax.rem(p, chunks) < split

    @staged(-AHEAD)
    def stage_offer(q):
        offer(q)

    @staged(0, chunks)
    def stage_weights(k):
        @pl.when(k + 1 < chunks)
        def _():
            for copy in up_copies(k + 1):
                copy.start()

        for copy in down_copies(k):
            copy.start()

    @staged(0)
    def stage_arrive(q):
        def both():
            arrive_near(q, 0, False)
            arrive_near(q, 1, False)

        either(gather_split(q), both, lambda: arrive_near(q, 0, True))

        @pl.when(q == chunks // 2)
        def _():
            route_local().wait()
            for step in range(1, zs):
                route_z(step).wait_recv()
            route_side(side).start()

    @staged(-SPLIT_AHEAD)
    def stage_split(q):
        def both():
            y_hop(q, other_side, z, 4).wait_recv()
            z_own(q, 1)

        either(gather_split(q), both, lambda: None)

    @staged(LAG_RELAY)
    def stage_relay(q):
        def both():
            arrive_far(q, 0, False)
            arrive_far(q, 1, False)
            core_hop(q, core, 0).start()
            core_hop(q, core, 1).start()

        def one():
            arrive_far(q, 0, True)
            core_hop(q, core, 0).start()

        either(gather_split(q), both, one)

    @staged(LAG_SIDE)
    def stage_side(q):
        def one():
            spot = xb.at[q, core, other_side]
            send(spot, spot, out_s.at[5], ay_r.at[q], side_dev).wait_recv()
            core_hop(q, core, 1).start()

        either(gather_split(q), lambda: None, one)

        @pl.when(q == chunks // 2)
        def _():
            route_side(other_side).wait_recv()
            route_core(core).start()

    @staged(LAG_USE)
    def stage_up(q):
        spot = xb.at[q, other_core]
        send(spot, spot, out_s.at[6], ac_r.at[q], core_dev).wait_recv()
        k = lax.rem(q, chunks)

        @pl.when(q < chunks)
        def _():
            up_wait(k)

        folded = xb[q].reshape(groups, size, CHUNK)
        moved = jnp.dot(perm[...], jnp.concatenate([folded[g] for g in range(groups)], axis=1), preferred_element_type=F32).astype(BF16)
        left = jnp.concatenate([
            jnp.concatenate([moved[f * unit:(f + 1) * unit, g * CHUNK:(g + 1) * CHUNK] for f in range(fold)], axis=1)
            for g in range(groups)
        ], axis=0)
        for e in range(EXP_G):
            acc[2 * e] += jnp.dot(left, wb[k, e], preferred_element_type=F32)
            acc[2 * e + 1] += jnp.dot(left, wb[k, EXP_G + e], preferred_element_type=F32)

        @pl.when(k == chunks - 1)
        def _():
            b = q // chunks

            @pl.when(b == 0)
            def _():
                route_core(other_core).wait_recv()

            line = iota_f32((1, units * pad_rows), 1)
            unit_of = floor_div(line, pad_rows)
            row_of = line - unit_of * pad_rows - (b * part).astype(F32)
            wanted = jnp.where((row_of >= 0) & (row_of < part), unit_of * part + row_of, -1.0)
            pick = one_hot(iota_f32((lines, units * pad_rows), 0) == wanted)
            scales = jnp.dot(pick, rb[...].reshape(units * pad_rows, LANES), preferred_element_type=F32)
            lane = lax.broadcasted_iota(jnp.int32, (lines, LANES), 1)
            first_expert = me // (wide // GROUPS) * EXP_G
            for e in range(EXP_G):
                scale = jnp.sum(jnp.where(lane == first_expert + e, scales, 0.0), axis=1, keepdims=True)
                gate = acc[2 * e]
                value = gate / (1.0 + jnp.exp(-gate)) * acc[2 * e + 1]
                hid[b, :, e * hidden:(e + 1) * hidden] = (value * scale).astype(BF16)
            acc[...] = jnp.zeros_like(acc)

    @staged(lag_down)
    def stage_down(p):
        k = lax.rem(p, chunks)

        @pl.when(p < chunks)
        def _():
            down_wait(k)

        down = jnp.dot(hid[p // chunks], wdb[k], preferred_element_type=F32).astype(BF16)
        stacked = jnp.concatenate([
            jnp.concatenate([down[g * unit:(g + 1) * unit, f * CHUNK:(f + 1) * CHUNK] for f in range(fold)], axis=0)
            for g in range(groups)
        ], axis=1)
        moved = jnp.dot(perm_back[...], stacked, preferred_element_type=F32).astype(BF16)
        flat = jnp.concatenate([moved[:, g * CHUNK:(g + 1) * CHUNK] for g in range(groups)], axis=0)
        packed[p] = flat.reshape(CORES, SIDES, zs, unit, CHUNK)
        back_core(p).start()

    @staged(lag_down + LAG_SUM)
    def stage_sum(p):
        back_core(p).wait_recv()
        for rel in (1, 0):
            red[p, rel] = (packed[p, core, halves[rel]].astype(F32) + got_core[p, halves[rel]].astype(F32)).astype(BF16)

        def both():
            reduce_first(p, 0)
            reduce_first(p, 1)

        either(scatter_split(p), both, lambda: back_side(p).start())

    @staged(lag_down + LAG_Z)
    def stage_z(p):
        def both():
            reduce_second(p, 0)
            reduce_second(p, 1)

        def one():
            back_side(p).wait_recv()
            red[p, 0] = (red[p, 0].astype(F32) + got_side[p].astype(F32)).astype(BF16)
            reduce_first(p, 0)

        either(scatter_split(p), both, one)

    @staged(lag_down + LAG_ZR)
    def stage_zr(p):
        def both():
            got_y[p, 0] = reduce_last(p, 1).astype(BF16)
            back_last(p).start()

        either(scatter_split(p), both, lambda: reduce_second(p, 0))

    @staged(lag_down + LAG_END)
    def stage_end(p):
        b = p // chunks
        k = lax.rem(p, chunks)
        spot = pl.ds(pl.multiple_of(b * unit, unit), unit)

        def both():
            back_last(p).wait_recv()
            fin[k, spot] = (reduce_last(p, 0) + got_y[p, 1].astype(F32)).astype(BF16)

        def one():
            fin[k, spot] = reduce_last(p, 0).astype(BF16)

        either(scatter_split(p), both, one)

        @pl.when(b == batches - 1)
        def _():
            out_of = one_hot(iota_f32((fold * pad_rows, held), 0) == place(iota_f32((1, held), 1)))
            flat = jnp.dot(out_of, fin[k], preferred_element_type=F32).astype(BF16)
            for f in range(fold):
                columns = pl.ds(pl.multiple_of(k * span + f * CHUNK, CHUNK), CHUNK)
                out_ref[:, columns] = flat[f * pad_rows:f * pad_rows + rows]

    @pl.loop(0, total + lag_down + LAG_END)
    def _(now):
        stage_weights(now)
        stage_offer(now)
        stage_arrive(now)
        stage_split(now)
        stage_relay(now)
        stage_side(now)
        stage_sum(now)
        stage_z(now)
        stage_zr(now)
        stage_end(now)
        stage_up(now)
        stage_down(now)

    def sent(kind, spot):
        send(spot, spot, out_s.at[kind], ay_r.at[0], core_dev).wait_send()

    plain = total - extra

    def sent_lines(kind, pairs, rule, ref):
        by_count(pairs, rule, lambda n: sent(kind, ref.at[:, 0, pl.ds(0, n)]))
        if extra:
            by_count(pairs, rule, lambda n: sent(kind + 1, ref.at[pl.ds(0, extra), 0, pl.ds(0, n)]))

    sent_lines(0, ends(near), any_end, red)
    sent_lines(2, ends(range(NEAR, zs - 1)), any_through, red)
    sent(4, red.at[:, 0, 0])
    sent(5, red.at[pl.ds(0, plain), 0, pl.ds(0, zs - 1)])
    sent(6, xb.at[:, 0])
    sent(7, packed.at[:, 0])
    sent(8, red.at[pl.ds(0, plain), 0])
    sent_lines(10, ends(near), any_end, red)
    sent_lines(12, ends(far), any_end, red)
    if extra:
        sent(9, got_y.at[pl.ds(0, extra), 0])
    spot = rb.at[0, 0, pl.ds(0, zs - 1)]
    send(spot, spot, route_s.at[0], route_r.at[0], core_dev).wait_send()
    route_side(side).wait_send()
    route_core(core).wait_send()


def local(wide, interpret, tokens, expert_ids, gates, w_gate, w_up, w_down):
    rows, model = tokens.shape
    hidden = w_gate.shape[2]
    batches = BATCHES if rows % BATCHES == 0 else 1
    part = rows // batches
    fold = 16 // math.gcd(16, part)
    span = fold * CHUNK
    chunks = model // span
    total = batches * chunks
    split = min(SPLIT, chunks)
    extra = batches * split
    zs = wide // (CORES * SIDES)
    pad_rows = -(-rows // 16) * 16
    unit = part * fold
    size = fold * unit
    lines = wide * part
    slots = 2 * min(NEAR, zs - 1)

    any_space = pl.BlockSpec(memory_space=pl.ANY)
    dma = pltpu.SemaphoreType.DMA
    out = pl.pallas_call(
        functools.partial(kernel, wide, rows, batches, fold, split),
        out_shape=jax.ShapeDtypeStruct((rows, model), BF16),
        in_specs=[any_space] + [pl.BlockSpec(memory_space=pltpu.VMEM)] * 2 + [any_space] * 3,
        out_specs=pl.BlockSpec(memory_space=pltpu.VMEM),
        scratch_shapes=[
            pltpu.VMEM((rows, model), BF16),
            pltpu.VMEM((pad_rows, model), BF16),
            pltpu.VMEM((pad_rows, LANES), BF16),
            pltpu.VMEM((total, CORES, SIDES, zs, unit, CHUNK), BF16),
            pltpu.VMEM((CORES, SIDES, zs, pad_rows, LANES), BF16),
            pltpu.VMEM((chunks, 2 * EXP_G, span, hidden), BF16),
            pltpu.VMEM((chunks, EXP_G * hidden, span), BF16),
            pltpu.VMEM((2 * EXP_G, lines, hidden), F32),
            pltpu.VMEM((batches, lines, EXP_G * hidden), BF16),
            pltpu.VMEM((size, size), BF16),
            pltpu.VMEM((size, size), BF16),
            pltpu.VMEM((total, CORES, SIDES, zs, unit, CHUNK), BF16),
            pltpu.VMEM((total, SIDES, zs, unit, CHUNK), BF16),
            pltpu.VMEM((total, SIDES, zs, unit, CHUNK), BF16),
            pltpu.VMEM((total, zs, unit, CHUNK), BF16),
            pltpu.VMEM((total, SIDES, slots, unit, CHUNK), BF16),
            pltpu.VMEM((total if zs - 1 > NEAR else 1, SIDES, zs, unit, CHUNK), BF16),
            pltpu.VMEM((total if split else 1, 2, unit, CHUNK), BF16),
            pltpu.VMEM((chunks, batches * unit, CHUNK), BF16),
            dma(()),
            dma(()),
            dma((chunks,)),
            dma((chunks,)),
            dma((3,)),
            dma((zs + 2,)),
            dma((14,)),
            dma((total + extra, slots)),
            dma((total + extra, zs - 1 - NEAR) if zs - 1 > NEAR else (1, 1)),
            dma((total,)),
            dma((total,)),
            dma((total,)),
            dma((total,)),
            dma((total + extra,)),
            dma((total + extra, zs - 1 - NEAR) if zs - 1 > NEAR else (1, 1)),
        ],
        compiler_params=pltpu.CompilerParams(collective_id=0, has_side_effects=True, vmem_limit_bytes=67043328),
        **interpret,
    )(tokens, expert_ids.T, gates.T, w_gate, w_up, w_down)
    return out


def solution(mesh, interpret=None):
    return jax.shard_map(
        functools.partial(local, mesh.shape["wide"], interpret or {}),
        mesh=mesh,
        in_specs=(
            P(("parts", "wide"), None),
            P(("parts", "wide"), None),
            P(("parts", "wide"), None),
            P(None, None, "wide"),
            P(None, None, "wide"),
            P(None, "wide", None),
        ),
        out_specs=P(("parts", "wide"), None),
        check_vma=False,
    )
```

time: 62.7 us -> 58.1 us (0.927)
  local copies, waits for them, and re-layouts: 4.36 us -> 1.64 us
  Pallas kernels: 58 us -> 56.3 us
    unnamed x3 -> x1, local copies, waits for them, and re-layouts: 4.36 us -> 1.64 us
    pallas_call x1, Pallas kernels: 58 us -> 56.3 us  [local(): pl.pallas_call(functools.partial(kernel, wide, rows, batches, fold, split...]
where the time goes in v1:
time: 58.1 us; the launch traced here: 57.9 us
  Pallas kernels  56.3 us (97%)
  local copies, waits for them, and re-layouts  1.64 us (3%)
    pallas_call x1, Pallas kernels, local(): pl.pallas_call(functools.partial(kernel, wide, rows, batches, fold, split...  56.3 us
    unnamed x1, local copies, waits for them, and re-layouts  1.64 us

profile of v1, /device:TPU:0, one launch (start us, length us, event | category | flops | bytes accessed | tf_op | source)
XLA Modules:
  0.0 57.9 jit_solution(14660117619965049201)
XLA Ops:
  0.0 56.3 %shard_map.64 = bf16[12,7168]{1,0:T(8,128)(2,1)} custom-call(bf16[12,7168]{1,0:T(8,128)(2,1)} %tok_ref.1, s32[8,12]{1,0:T(8,128)} %bitcast.2, f32[8,12]{1,0:T(8,128)} %bitcast.3, bf16[2,7168,512]{2,1,0:T(8,128)(2,1)} %wg_ref.1, bf16[2,7168,512]{2,1,0:T(8,128)(2,1)} %wu_ref.1, bf16[2,512,7168]{2,1,0:T(8,128)(2,1)} %wd_ref.1), custom_call_target="tpu_custom_call" | custom-call | tf_op jit(solution)/shard_map/pallas_call | solution.py:596
  56.3 1.6 %copy.8 = bf16[12,7168]{1,0:T(8,128)(2,1)} copy(bf16[12,7168]{1,0:T(8,128)(2,1)} %shard_map.64) | data formatting | bytes 344064

commit v2 on v1

--- a/solution.py
+++ b/solution.py
@@ -18,14 +18,14 @@
 SPLIT = 0
 AHEAD = 20
 SPLIT_AHEAD = 0
-LAG_RELAY = 0
-LAG_SIDE = 2
-LAG_USE = 3
+LAG_RELAY = 2
+LAG_SIDE = 4
+LAG_USE = 5
 LAG_SUM = 2
-LAG_Z = 5
-LAG_ZR = 5
-LAG_END = 8
-NEAR = 3
+LAG_Z = 4
+LAG_ZR = 6
+LAG_END = 10
+NEAR = 2
 F32 = jnp.float32
 BF16 = jnp.bfloat16
 
@@ -46,7 +46,7 @@
     wide, rows, batches, fold, split,
     tok_ref, ids_ref, gate_ref, wg_ref, wu_ref, wd_ref, out_ref,
     tok, padded, r_ref, xb, rb, wb, wdb, acc, hid, perm, perm_back, packed, got_core, red, got_side, got_z, relay, got_y, fin,
-    tok_sem, own_sem, w_sem, d_sem, route_s, route_r, out_s, az_r, af_r, ay_r, ac_r, bc_r, by_r, bz_r, br_r,
+    tok_sem, own_sem, w_sem, d_sem, route_s, route_r, out_s, az_r, af_r, ay_r, ac_r, bc_r, by_r, bo_r, bz_r, br_r,
 ):
     zs = wide // (CORES * SIDES)
     total = xb.shape[0]
@@ -204,8 +204,11 @@
     def back_core(p):
         return send(packed.at[p, other_core], got_core.at[p], out_s.at[7], bc_r.at[p], core_dev)
 
-    def back_side(p):
-        return send(red.at[p, 1], got_side.at[p], out_s.at[8], by_r.at[p], side_dev)
+    def back_side(p, dst):
+        return send(red.at[p, 1, dst], got_side.at[p, dst], out_s.at[8], by_r.at[p], side_dev)
+
+    def back_own(p):
+        return send(red.at[p, 1, z], got_side.at[p, z], out_s.at[14], bo_r.at[p], side_dev)
 
     def back_last(p):
         return send(got_y.at[p, 0], got_y.at[p, 1], out_s.at[9], by_r.at[p], side_dev)
@@ -485,7 +488,19 @@
             reduce_first(p, 0)
             reduce_first(p, 1)
 
-        either(scatter_split(p), both, lambda: back_side(p).start())
+        def one():
+            for d, sign, dst, slot in reversed(around(range(1, zs))):
+                @pl.when(inside(dst))
+                def _():
+                    back_side(p, dst).start()
+
+        either(scatter_split(p), both, one)
+
+        @pl.when(p == total - 1)
+        def _():
+            @pl.loop(0, total)
+            def _(j):
+                either(scatter_split(j), lambda: None, lambda: back_own(j).start())
 
     @staged(lag_down + LAG_Z)
     def stage_z(p):
@@ -494,8 +509,11 @@
             reduce_second(p, 1)
 
         def one():
-            back_side(p).wait_recv()
-            red[p, 0] = (red[p, 0].astype(F32) + got_side[p].astype(F32)).astype(BF16)
+            spot = got_side.at[p, pl.ds(0, zs - 1)]
+            send(spot, spot, out_s.at[8], by_r.at[p], side_dev).wait_recv()
+            for step in range(1, zs):
+                dst = lax.rem(z + step, zs)
+                red[p, 0, dst] = (red[p, 0, dst].astype(F32) + got_side[p, dst].astype(F32)).astype(BF16)
             reduce_first(p, 0)
 
         either(scatter_split(p), both, one)
@@ -519,7 +537,8 @@
             fin[k, spot] = (reduce_last(p, 0) + got_y[p, 1].astype(F32)).astype(BF16)
 
         def one():
-            fin[k, spot] = reduce_last(p, 0).astype(BF16)
+            back_own(p).wait_recv()
+            fin[k, spot] = (reduce_last(p, 0) + got_side[p, z].astype(F32)).astype(BF16)
 
         either(scatter_split(p), both, one)
 
@@ -562,7 +581,8 @@
     sent(5, red.at[pl.ds(0, plain), 0, pl.ds(0, zs - 1)])
     sent(6, xb.at[:, 0])
     sent(7, packed.at[:, 0])
-    sent(8, red.at[pl.ds(0, plain), 0])
+    sent(8, red.at[pl.ds(0, plain), 0, pl.ds(0, zs - 1)])
+    sent(14, red.at[pl.ds(0, plain), 0, 0])
     sent_lines(10, ends(near), any_end, red)
     sent_lines(12, ends(far), any_end, red)
     if extra:
@@ -624,9 +644,10 @@
             dma((chunks,)),
             dma((3,)),
             dma((zs + 2,)),
-            dma((14,)),
+            dma((15,)),
             dma((total + extra, slots)),
             dma((total + extra, zs - 1 - NEAR) if zs - 1 > NEAR else (1, 1)),
+            dma((total,)),
             dma((total,)),
             dma((total,)),
             dma((total,)),

time: 58.1 us -> 55.8 us (0.960)
  Pallas kernels: 56.3 us -> 53.9 us
    pallas_call x1, Pallas kernels: 56.3 us -> 53.9 us  [local(): pl.pallas_call(functools.partial(kernel, wide, rows, batches, fold, split...]
where the time goes in v2:
time: 55.8 us; the launch traced here: 55.6 us
  Pallas kernels  53.9 us (97%)
  local copies, waits for them, and re-layouts  1.64 us (3%)
    pallas_call x1, Pallas kernels, local(): pl.pallas_call(functools.partial(kernel, wide, rows, batches, fold, split...  53.9 us
    unnamed x1, local copies, waits for them, and re-layouts  1.64 us

profile of v2, /device:TPU:0, one launch (start us, length us, event | category | flops | bytes accessed | tf_op | source)
XLA Modules:
  0.0 55.6 jit_solution(9619034979278739321)
XLA Ops:
  0.0 53.9 %shard_map.64 = bf16[12,7168]{1,0:T(8,128)(2,1)} custom-call(bf16[12,7168]{1,0:T(8,128)(2,1)} %tok_ref.1, s32[8,12]{1,0:T(8,128)} %bitcast.2, f32[8,12]{1,0:T(8,128)} %bitcast.3, bf16[2,7168,512]{2,1,0:T(8,128)(2,1)} %wg_ref.1, bf16[2,7168,512]{2,1,0:T(8,128)(2,1)} %wu_ref.1, bf16[2,512,7168]{2,1,0:T(8,128)(2,1)} %wd_ref.1), custom_call_target="tpu_custom_call" | custom-call | tf_op jit(solution)/shard_map/pallas_call | solution.py:616
  53.9 1.6 %copy.8 = bf16[12,7168]{1,0:T(8,128)(2,1)} copy(bf16[12,7168]{1,0:T(8,128)(2,1)} %shard_map.64) | data formatting | bytes 344064

commit v3 on v2

--- a/solution.py
+++ b/solution.py
@@ -15,9 +15,10 @@
 LANES = 128
 CHUNK = 256
 BATCHES = 1
-SPLIT = 0
+SPLIT_IN = 1
+SPLIT_OUT = 0
 AHEAD = 20
-SPLIT_AHEAD = 0
+SPLIT_AHEAD = 4
 LAG_RELAY = 2
 LAG_SIDE = 4
 LAG_USE = 5
@@ -43,9 +44,9 @@
 
 
 def kernel(
-    wide, rows, batches, fold, split,
+    wide, rows, batches, fold, split_in, split_out,
     tok_ref, ids_ref, gate_ref, wg_ref, wu_ref, wd_ref, out_ref,
-    tok, padded, r_ref, xb, rb, wb, wdb, acc, hid, perm, perm_back, packed, got_core, red, got_side, got_z, relay, got_y, fin,
+    tok, r_ref, xb, rb, wb, wdb, acc, hid, perm, perm_back, packed, got_core, red, got_side, got_z, relay, got_y, fin, scale_ref, out_v,
     tok_sem, own_sem, w_sem, d_sem, route_s, route_r, out_s, az_r, af_r, ay_r, ac_r, bc_r, by_r, bo_r, bz_r, br_r,
 ):
     zs = wide // (CORES * SIDES)
@@ -62,7 +63,8 @@
     pad_rows = r_ref.shape[0]
     near = range(1, min(NEAR, zs - 1) + 1)
     far = range(NEAR + 1, zs)
-    extra = batches * split
+    extra_in = batches * split_in
+    extra_out = batches * split_out
 
     me = lax.axis_index("wide")
     core = lax.rem(me, CORES)
@@ -110,8 +112,11 @@
     def down_wait(k):
         pltpu.make_async_copy(wdb.at[k], wdb.at[k], d_sem.at[k]).wait()
 
-    def line_of(q, rel, first):
-        return q if rel == 0 else total + q // chunks * split + lax.rem(q, chunks) - first
+    def line_in(q, rel):
+        return q if rel == 0 else total + q // chunks * split_in + lax.rem(q, chunks) - (chunks - split_in)
+
+    def line_out(p, rel):
+        return p if rel == 0 else total + p // chunks * split_out + lax.rem(p, chunks)
 
     def by_count(pairs, rule, act):
         here = sum(rule(z + sign * d, z - sign).astype(jnp.int32) for d, sign in pairs)
@@ -146,7 +151,7 @@
         return send(spot, spot, out_s.at[6], ac_r.at[q], core_dev)
 
     def z_own(q, rel):
-        line = line_of(q, rel, chunks - split)
+        line = line_in(q, rel)
         for d, sign, dst, slot in reversed(around(near)):
             @pl.when(inside(dst))
             def _():
@@ -159,7 +164,7 @@
                 if d >= NEAR and d + 1 < zs:
                     @pl.when(inside(z - sign))
                     def _():
-                        z_hop(q, rel, src, z - sign, 2 + rel, af_r.at[line_of(q, rel, chunks - split), d - NEAR]).start()
+                        z_hop(q, rel, src, z - sign, 2 + rel, af_r.at[line_in(q, rel), d - NEAR]).start()
                 if onward:
                     y_hop(q, side, src, 5).start()
 
@@ -171,7 +176,7 @@
         by_count(ends(distances), any_end, wait)
 
     def arrive_near(q, rel, onward):
-        line = line_of(q, rel, chunks - split)
+        line = line_in(q, rel)
         for d, sign, src, slot in around(near):
             @pl.when(inside(z - sign * d))
             def _():
@@ -185,7 +190,7 @@
 
     def arrive_far(q, rel, onward):
         for d in far:
-            z_wait(q, rel, [d], af_r.at[line_of(q, rel, chunks - split), d - NEAR - 1])
+            z_wait(q, rel, [d], af_r.at[line_in(q, rel), d - NEAR - 1])
             z_onward(q, rel, [d], onward)
 
     def route_z(step):
@@ -214,11 +219,11 @@
         return send(got_y.at[p, 0], got_y.at[p, 1], out_s.at[9], by_r.at[p], side_dev)
 
     def back_z(p, rel, dst, slot):
-        r_sem = bz_r.at[line_of(p, rel, 0)]
+        r_sem = bz_r.at[line_out(p, rel)]
         return send(red.at[p, rel, dst], got_z.at[p, rel, slot], out_s.at[10 + rel], r_sem, at(dst, side, core))
 
     def back_relay(p, rel, d, dst, to):
-        r_sem = br_r.at[line_of(p, rel, 0), d]
+        r_sem = br_r.at[line_out(p, rel), d]
         return send(red.at[p, rel, dst], relay.at[p, rel, dst], out_s.at[12 + rel], r_sem, at(to, side, core))
 
     def reduce_out(p, rel, d, sign, dst, slot):
@@ -239,7 +244,7 @@
         for d in reversed(range(NEAR, zs - 1)):
             def wait(n):
                 spot = relay.at[p, rel, pl.ds(0, n)]
-                send(spot, spot, out_s.at[0], br_r.at[line_of(p, rel, 0), d - NEAR], core_dev).wait_recv()
+                send(spot, spot, out_s.at[0], br_r.at[line_out(p, rel), d - NEAR], core_dev).wait_recv()
 
             by_count(ends([d]), any_through, wait)
             for _, sign, dst, slot in around([d]):
@@ -251,7 +256,7 @@
     def reduce_last(p, rel):
         def wait(n):
             spot = got_z.at[p, rel, pl.ds(0, n)]
-            send(spot, spot, out_s.at[0], bz_r.at[line_of(p, rel, 0)], core_dev).wait_recv()
+            send(spot, spot, out_s.at[0], bz_r.at[line_out(p, rel)], core_dev).wait_recv()
 
         by_count(ends(near), any_end, wait)
         done = red[p, rel, z].astype(F32)
@@ -264,14 +269,6 @@
     for copy in up_copies(0):
         copy.start()
 
-    for d, sign, src, slot in around(near):
-        @pl.when(jnp.logical_not(inside(z - sign * d)))
-        def _():
-            @pl.loop(0, total)
-            def _(p):
-                for rel in range(SIDES):
-                    got_z[p, rel, slot] = jnp.zeros((unit, CHUNK), BF16)
-
     barrier = pltpu.get_barrier_semaphore()
     for step in range(1, zs):
         pl.semaphore_signal(barrier, inc=1, device_id=at(lax.rem(z + step, zs), side, core), device_id_type=pl.DeviceIdType.MESH)
@@ -287,25 +284,25 @@
     held = batches * unit
     into = one_hot(iota_f32((held, fold * pad_rows), 1) == place(iota_f32((held, 1), 0)))
     spread = one_hot(iota_f32((pad_rows, rows), 0) == iota_f32((pad_rows, rows), 1))
-    token_copy.wait()
-    padded[...] = jnp.dot(spread, tok[...], preferred_element_type=F32).astype(BF16)
-
-    def pack(k):
-        tiles = jnp.concatenate([padded[:, k * span + f * CHUNK:k * span + (f + 1) * CHUNK] for f in range(fold)], axis=0)
-        mine = jnp.dot(into, tiles, preferred_element_type=F32).astype(BF16)
-        for b in range(batches):
-            xb[b * chunks + k, core, side, z] = mine[b * unit:(b + 1) * unit]
-
-    def offer(q):
-        y_hop(q, side, z, 4).start()
-        z_own(q, 0)
-
     token = lax.broadcasted_iota(jnp.int32, (LANES, rows), 0)
     route = jnp.zeros((LANES, rows), F32)
     for slot in range(ids_ref.shape[0]):
         route = route + jnp.where(ids_ref[slot:slot + 1, :] == token, gate_ref[slot:slot + 1, :], 0.0)
     r_ref[...] = lax.dot_general(spread, route.astype(BF16), (((1,), (1,)), ((), ())), preferred_element_type=F32).astype(BF16)
     route_local().start()
+    token_copy.wait()
+
+    def pack(k):
+        padded = jnp.dot(spread, tok[:, k * span:(k + 1) * span], preferred_element_type=F32).astype(BF16)
+        tiles = jnp.concatenate([padded[:, f * CHUNK:(f + 1) * CHUNK] for f in range(fold)], axis=0)
+        mine = jnp.dot(into, tiles, preferred_element_type=F32).astype(BF16)
+        for b in range(batches):
+            xb[b * chunks + k, core, side, z] = mine[b * unit:(b + 1) * unit]
+
+    def offer(q):
+        y_hop(q, side, z, 4).start()
+        z_own(q, 0)
+
     pack(0)
     pl.semaphore_wait(barrier, zs + 1)
     offer(0)
@@ -318,6 +315,14 @@
     for q in range(chunks, min(AHEAD, total)):
         offer(q)
 
+    for d, sign, src, slot in around(near):
+        @pl.when(jnp.logical_not(inside(z - sign * d)))
+        def _():
+            @pl.loop(0, total)
+            def _(p):
+                for rel in range(SIDES if split_out else 1):
+                    got_z[p, rel, slot] = jnp.zeros((unit, CHUNK), BF16)
+
     def order(index):
         first = floor_div(index, unit)
         rest = index - first * unit
@@ -340,17 +345,17 @@
         return wrap
 
     def either(test, yes, no):
-        if split == 0:
+        if test is None:
             no()
         else:
             pl.when(test)(yes)
             pl.when(jnp.logical_not(test))(no)
 
     def gather_split(q):
-        return lax.rem(q, chunks) >= chunks - split
+        return lax.rem(q, chunks) >= chunks - split_in if split_in else None
 
     def scatter_split(p):
-        return lax.rem(p, chunks) < split
+        return lax.rem(p, chunks) < split_out if split_out else None
 
     @staged(-AHEAD)
     def stage_offer(q):
@@ -437,7 +442,7 @@
             acc[2 * e] += jnp.dot(left, wb[k, e], preferred_element_type=F32)
             acc[2 * e + 1] += jnp.dot(left, wb[k, EXP_G + e], preferred_element_type=F32)
 
-        @pl.when(k == chunks - 1)
+        @pl.when(k == max(chunks - 3, chunks // 2))
         def _():
             b = q // chunks
 
@@ -455,10 +460,19 @@
             first_expert = me // (wide // GROUPS) * EXP_G
             for e in range(EXP_G):
                 scale = jnp.sum(jnp.where(lane == first_expert + e, scales, 0.0), axis=1, keepdims=True)
+                scale_ref[e] = jnp.broadcast_to(scale, (lines, LANES))
+
+        @pl.when(k == chunks - 1)
+        def _():
+            b = q // chunks
+
+            for e in range(EXP_G):
+                scale = scale_ref[e][:, :1]
                 gate = acc[2 * e]
                 value = gate / (1.0 + jnp.exp(-gate)) * acc[2 * e + 1]
                 hid[b, :, e * hidden:(e + 1) * hidden] = (value * scale).astype(BF16)
-            acc[...] = jnp.zeros_like(acc)
+            if batches > 1:
+                acc[...] = jnp.zeros_like(acc)
 
     @staged(lag_down)
     def stage_down(p):
@@ -548,16 +562,18 @@
             flat = jnp.dot(out_of, fin[k], preferred_element_type=F32).astype(BF16)
             for f in range(fold):
                 columns = pl.ds(pl.multiple_of(k * span + f * CHUNK, CHUNK), CHUNK)
-                out_ref[:, columns] = flat[f * pad_rows:f * pad_rows + rows]
+                out_v[:, columns] = flat[f * pad_rows:f * pad_rows + rows]
+            columns = pl.ds(pl.multiple_of(k * span, span), span)
+            pltpu.make_async_copy(out_v.at[:, columns], out_ref.at[:, columns], tok_sem).start()
 
     @pl.loop(0, total + lag_down + LAG_END)
     def _(now):
-        stage_weights(now)
         stage_offer(now)
         stage_arrive(now)
         stage_split(now)
         stage_relay(now)
         stage_side(now)
+        stage_weights(now)
         stage_sum(now)
         stage_z(now)
         stage_zr(now)
@@ -568,25 +584,24 @@
     def sent(kind, spot):
         send(spot, spot, out_s.at[kind], ay_r.at[0], core_dev).wait_send()
 
-    plain = total - extra
-
-    def sent_lines(kind, pairs, rule, ref):
-        by_count(pairs, rule, lambda n: sent(kind, ref.at[:, 0, pl.ds(0, n)]))
+    pltpu.make_async_copy(out_v, out_ref, tok_sem).wait()
+    def sent_lines(kind, pairs, rule, extra):
+        by_count(pairs, rule, lambda n: sent(kind, red.at[:, 0, pl.ds(0, n)]))
         if extra:
-            by_count(pairs, rule, lambda n: sent(kind + 1, ref.at[pl.ds(0, extra), 0, pl.ds(0, n)]))
-
-    sent_lines(0, ends(near), any_end, red)
-    sent_lines(2, ends(range(NEAR, zs - 1)), any_through, red)
+            by_count(pairs, rule, lambda n: sent(kind + 1, red.at[pl.ds(0, extra), 0, pl.ds(0, n)]))
+
+    sent_lines(0, ends(near), any_end, extra_in)
+    sent_lines(2, ends(range(NEAR, zs - 1)), any_through, extra_in)
     sent(4, red.at[:, 0, 0])
-    sent(5, red.at[pl.ds(0, plain), 0, pl.ds(0, zs - 1)])
+    sent(5, red.at[pl.ds(0, total - extra_in), 0, pl.ds(0, zs - 1)])
     sent(6, xb.at[:, 0])
     sent(7, packed.at[:, 0])
-    sent(8, red.at[pl.ds(0, plain), 0, pl.ds(0, zs - 1)])
-    sent(14, red.at[pl.ds(0, plain), 0, 0])
-    sent_lines(10, ends(near), any_end, red)
-    sent_lines(12, ends(far), any_end, red)
-    if extra:
-        sent(9, got_y.at[pl.ds(0, extra), 0])
+    sent(8, red.at[pl.ds(0, total - extra_out), 0, pl.ds(0, zs - 1)])
+    sent(14, red.at[pl.ds(0, total - extra_out), 0, 0])
+    sent_lines(10, ends(near), any_end, extra_out)
+    sent_lines(12, ends(far), any_end, extra_out)
+    if extra_out:
+        sent(9, got_y.at[pl.ds(0, extra_out), 0])
     spot = rb.at[0, 0, pl.ds(0, zs - 1)]
     send(spot, spot, route_s.at[0], route_r.at[0], core_dev).wait_send()
     route_side(side).wait_send()
@@ -602,8 +617,8 @@
     span = fold * CHUNK
     chunks = model // span
     total = batches * chunks
-    split = min(SPLIT, chunks)
-    extra = batches * split
+    split_in, split_out = min(SPLIT_IN, chunks), min(SPLIT_OUT, chunks)
+    extra = batches * max(split_in, split_out)
     zs = wide // (CORES * SIDES)
     pad_rows = -(-rows // 16) * 16
     unit = part * fold
@@ -614,13 +629,12 @@
     any_space = pl.BlockSpec(memory_space=pl.ANY)
     dma = pltpu.SemaphoreType.DMA
     out = pl.pallas_call(
-        functools.partial(kernel, wide, rows, batches, fold, split),
+        functools.partial(kernel, wide, rows, batches, fold, split_in, split_out),
         out_shape=jax.ShapeDtypeStruct((rows, model), BF16),
         in_specs=[any_space] + [pl.BlockSpec(memory_space=pltpu.VMEM)] * 2 + [any_space] * 3,
-        out_specs=pl.BlockSpec(memory_space=pltpu.VMEM),
+        out_specs=any_space,
         scratch_shapes=[
             pltpu.VMEM((rows, model), BF16),
-            pltpu.VMEM((pad_rows, model), BF16),
             pltpu.VMEM((pad_rows, LANES), BF16),
             pltpu.VMEM((total, CORES, SIDES, zs, unit, CHUNK), BF16),
             pltpu.VMEM((CORES, SIDES, zs, pad_rows, LANES), BF16),
@@ -636,8 +650,10 @@
             pltpu.VMEM((total, zs, unit, CHUNK), BF16),
             pltpu.VMEM((total, SIDES, slots, unit, CHUNK), BF16),
             pltpu.VMEM((total if zs - 1 > NEAR else 1, SIDES, zs, unit, CHUNK), BF16),
-            pltpu.VMEM((total if split else 1, 2, unit, CHUNK), BF16),
+            pltpu.VMEM((total if split_out else 1, 2, unit, CHUNK), BF16),
             pltpu.VMEM((chunks, batches * unit, CHUNK), BF16),
+            pltpu.VMEM((EXP_G, lines, LANES), F32),
+            pltpu.VMEM((rows, model), BF16),
             dma(()),
             dma(()),
             dma((chunks,)),

time: 55.8 us -> 55.5 us (level)
  no operation moved by 1% of the time
where the time goes in v3:
time: 55.5 us; the launch traced here: 55.3 us
  Pallas kernels  53.6 us (97%)
  local copies, waits for them, and re-layouts  1.64 us (3%)
    pallas_call x1, Pallas kernels, local(): pl.pallas_call(functools.partial(kernel, wide, rows, batches, fold, split...  53.6 us
    unnamed x1, local copies, waits for them, and re-layouts  1.64 us

profile of v3, /device:TPU:0, one launch (start us, length us, event | category | flops | bytes accessed | tf_op | source)
XLA Modules:
  0.0 55.3 jit_solution(5363431526668658877)
XLA Ops:
  0.0 53.6 %shard_map.64 = bf16[12,7168]{1,0:T(8,128)(2,1)} custom-call(bf16[12,7168]{1,0:T(8,128)(2,1)} %tok_ref.1, s32[8,12]{1,0:T(8,128)} %bitcast.2, f32[8,12]{1,0:T(8,128)} %bitcast.3, bf16[2,7168,512]{2,1,0:T(8,128)(2,1)} %wg_ref.1, bf16[2,7168,512]{2,1,0:T(8,128)(2,1)} %wu_ref.1, bf16[2,512,7168]{2,1,0:T(8,128)(2,1)} %wd_ref.1), custom_call_target="tpu_custom_call" | custom-call | tf_op jit(solution)/shard_map/pallas_call | solution.py:631
  53.6 1.6 %copy.8 = bf16[12,7168]{1,0:T(8,128)(2,1)} copy(bf16[12,7168]{1,0:T(8,128)(2,1)} %shard_map.64) | data formatting | bytes 344064

commit v4 on v3

--- a/solution.py
+++ b/solution.py
@@ -155,7 +155,7 @@
         for d, sign, dst, slot in reversed(around(near)):
             @pl.when(inside(dst))
             def _():
-                z_hop(q, rel, z, dst, rel, az_r.at[line, slot]).start()
+                z_hop(q, rel, z, dst, rel, az_r.at[line]).start()
 
     def z_onward(q, rel, distances, onward):
         for d, sign, src, slot in around(distances):
@@ -176,17 +176,8 @@
         by_count(ends(distances), any_end, wait)
 
     def arrive_near(q, rel, onward):
-        line = line_in(q, rel)
-        for d, sign, src, slot in around(near):
-            @pl.when(inside(z - sign * d))
-            def _():
-                z_hop(q, rel, z - sign * d, z - sign * d, 0, az_r.at[line, slot]).wait_recv()
-                if d >= NEAR and d + 1 < zs:
-                    @pl.when(inside(z + sign))
-                    def _():
-                        z_hop(q, rel, z - sign * d, z + sign, 2 + rel, af_r.at[line, d - NEAR]).start()
-                if onward:
-                    y_hop(q, side, z - sign * d, 5).start()
+        z_wait(q, rel, near, az_r.at[line_in(q, rel)])
+        z_onward(q, rel, near, onward)
 
     def arrive_far(q, rel, onward):
         for d in far:
@@ -213,7 +204,7 @@
         return send(red.at[p, 1, dst], got_side.at[p, dst], out_s.at[8], by_r.at[p], side_dev)
 
     def back_own(p):
-        return send(red.at[p, 1, z], got_side.at[p, z], out_s.at[14], bo_r.at[p], side_dev)
+        return send(red.at[p, 1, z], got_side.at[p, z], out_s.at[14], bo_r, side_dev)
 
     def back_last(p):
         return send(got_y.at[p, 0], got_y.at[p, 1], out_s.at[9], by_r.at[p], side_dev)
@@ -542,6 +533,11 @@
 
     @staged(lag_down + LAG_END)
     def stage_end(p):
+        @pl.when(p == 0)
+        def _():
+            spot = got_side.at[pl.ds(0, total - extra_out), 0]
+            send(spot, spot, out_s.at[14], bo_r, side_dev).wait_recv()
+
         b = p // chunks
         k = lax.rem(p, chunks)
         spot = pl.ds(pl.multiple_of(b * unit, unit), unit)
@@ -551,7 +547,6 @@
             fin[k, spot] = (reduce_last(p, 0) + got_y[p, 1].astype(F32)).astype(BF16)
 
         def one():
-            back_own(p).wait_recv()
             fin[k, spot] = (reduce_last(p, 0) + got_side[p, z].astype(F32)).astype(BF16)
 
         either(scatter_split(p), both, one)
@@ -577,9 +572,9 @@
         stage_sum(now)
         stage_z(now)
         stage_zr(now)
-        stage_end(now)
         stage_up(now)
         stage_down(now)
+        stage_end(now)
 
     def sent(kind, spot):
         send(spot, spot, out_s.at[kind], ay_r.at[0], core_dev).wait_send()
@@ -661,13 +656,13 @@
             dma((3,)),
             dma((zs + 2,)),
             dma((15,)),
-            dma((total + extra, slots)),
+            dma((total + extra,)),
             dma((total + extra, zs - 1 - NEAR) if zs - 1 > NEAR else (1, 1)),
             dma((total,)),
             dma((total,)),
             dma((total,)),
             dma((total,)),
-            dma((total,)),
+            dma(()),
             dma((total + extra,)),
             dma((total + extra, zs - 1 - NEAR) if zs - 1 > NEAR else (1, 1)),
         ],

time: 55.5 us -> 56.1 us (1.011)
  Pallas kernels: 53.6 us -> 54.2 us
    pallas_call x1, Pallas kernels: 53.6 us -> 54.2 us  [local(): pl.pallas_call(functools.partial(kernel, wide, rows, batches, fold, split...]
where the time goes in v4:
time: 56.1 us; the launch traced here: 55.9 us
  Pallas kernels  54.2 us (97%)
  local copies, waits for them, and re-layouts  1.64 us (3%)
    pallas_call x1, Pallas kernels, local(): pl.pallas_call(functools.partial(kernel, wide, rows, batches, fold, split...  54.2 us
    unnamed x1, local copies, waits for them, and re-layouts  1.64 us

profile of v4, /device:TPU:0, one launch (start us, length us, event | category | flops | bytes accessed | tf_op | source)
XLA Modules:
  0.0 55.9 jit_solution(8962624204114088372)
XLA Ops:
  0.0 54.2 %shard_map.64 = bf16[12,7168]{1,0:T(8,128)(2,1)} custom-call(bf16[12,7168]{1,0:T(8,128)(2,1)} %tok_ref.1, s32[8,12]{1,0:T(8,128)} %bitcast.2, f32[8,12]{1,0:T(8,128)} %bitcast.3, bf16[2,7168,512]{2,1,0:T(8,128)(2,1)} %wg_ref.1, bf16[2,7168,512]{2,1,0:T(8,128)(2,1)} %wu_ref.1, bf16[2,512,7168]{2,1,0:T(8,128)(2,1)} %wd_ref.1), custom_call_target="tpu_custom_call" | custom-call | tf_op jit(solution)/shard_map/pallas_call | solution.py:626
  54.2 1.6 %copy.8 = bf16[12,7168]{1,0:T(8,128)(2,1)} copy(bf16[12,7168]{1,0:T(8,128)(2,1)} %shard_map.64) | data formatting | bytes 344064
